TPU v7x, 128 devices: a whole 4x4x4 slice. The times are simulated.
128 devices in a mesh: view: 16 (over y, z), depth: 8 (over x, core).
Axes of the slice: x: 4, y: 4, z: 4, core: 2. Of those that a mesh axis runs over, the one named last changes fastest.
Arguments:
- features: bfloat16 [48, 1024, 32], P('view'), may hold values from -6 to 6
- view_lists: int32 [48, 10], P('view'), may hold values from 0 to 31
- requests: int32 [16, 16, 2], replicated, may hold values from 0 to 2
- warp_idx: int32 [48, 10, 64, 8, 128], P('view', None, None, 'depth'), may hold values from -682 to 1023
- conv_weight: bfloat16 [27, 8, 8], replicated, may hold values from -0.4375 to 0.4375
Outputs:
- regularized: bfloat16 [48, 8, 64, 8, 128], P('view', None, 'depth')
Inputs may be any that keep to these rules, and one draw needn't show every extreme that they name: `warp_idx`: A negative entry marks a sample that falls outside the source tile and is left out of the sum and the count.
All inputs are finite; a program needn't handle non-finite values.
Results may differ from a plain program's by a relative error of at most 0.0049.
Values may be sent and summed in bfloat16 or wider, within the bound.
No kernel may reach another device: no remote copies, remote signals or barrier semaphores. Data moves between devices by JAX's collectives and lax.ppermute only.
A program may use at most 128 MiB of HBM per device.

v0:
```python
import jax
import jax.numpy as jnp
from jax import lax
from jax.sharding import PartitionSpec as P


def padded_2(cells, sides, width):
    for axis, dim in sides:
        count = lax.axis_size(axis)
        ends = count - 1
        head = lax.slice_in_dim(cells, 0, width, axis=dim)
        tail = lax.slice_in_dim(cells, cells.shape[dim] - width, cells.shape[dim], axis=dim)
        cells = jnp.concatenate(
            [
                lax.ppermute(tail, axis, [(i, (i + 1) % count) for i in range(ends)]),
                cells,
                lax.ppermute(head, axis, [((i + 1) % count, i) for i in range(ends)]),
            ],
            axis=dim,
        )
    return cells


def mix_taps(padded, conv_weight, depth_out, rows_out, cols_out):
    summed = None
    for depth_tap in range(3):
        for row_tap in range(3):
            for col_tap in range(3):
                shifted = padded[
                    :,
                    :,
                    depth_tap : depth_tap + depth_out,
                    row_tap : row_tap + rows_out,
                    col_tap : col_tap + cols_out,
                ]
                kernel = conv_weight[9 * depth_tap + 3 * row_tap + col_tap]
                term = jnp.einsum(
                    "vgdhw,gk->vkdhw", shifted, kernel, preferred_element_type=jnp.float32
                )
                summed = term if summed is None else summed + term
    return summed


def on_device(features, view_lists, requests, warp_idx, conv_weight):
    view_here = lax.axis_index("view")
    depth_here = lax.axis_index("depth")
    depth_count = lax.axis_size("depth")
    local_views = features.shape[0]
    pixels = features.shape[1]
    channels = features.shape[2]
    sources = warp_idx.shape[1]
    planes = warp_idx.shape[2]
    row_count = warp_idx.shape[3]
    columns = warp_idx.shape[4]
    groups = conv_weight.shape[1]
    asked = requests.shape[2]
    tile_pool = lax.all_gather(features, "view", axis=0, tiled=True)
    owner_dev = view_lists // asked
    slot_index = view_lists % asked
    source_ids = owner_dev * local_views + requests[view_here, owner_dev, slot_index]
    flat_pool = tile_pool.reshape(-1, channels)
    own_pixels = row_count * columns
    own_rows = lax.dynamic_slice_in_dim(features, depth_here * own_pixels, own_pixels, 1)

    def one_view(item):
        own_tile, warp_rows, view_sources = item
        usable = (warp_rows >= 0).reshape(sources, planes, own_pixels)
        picks = view_sources[:, None, None, None] * pixels + jnp.maximum(warp_rows, 0)
        warped = jnp.take(flat_pool, picks.reshape(-1), axis=0)
        warped = warped.reshape(sources, planes, own_pixels, groups, channels // groups)
        own_groups = own_tile.reshape(own_pixels, groups, channels // groups)
        products = jnp.einsum(
            "sdpgk,pgk->sdpg", warped, own_groups, preferred_element_type=jnp.float32
        )
        masked = jnp.where(usable[..., None], products, jnp.float32(0.0))
        live_count = jnp.sum(usable.astype(jnp.float32), axis=0)
        corr = 0.5 * jnp.sum(masked, axis=0) / jnp.maximum(live_count, jnp.float32(1.0))[..., None]
        corr = jnp.transpose(corr, (2, 0, 1)).reshape(groups, planes, row_count, columns)
        return corr.astype(jnp.bfloat16)

    cost_rows = lax.map(one_view, (own_rows, warp_idx, source_ids))
    slab_planes = planes // depth_count
    slab = lax.all_to_all(cost_rows, "depth", split_axis=2, concat_axis=3, tiled=True)
    rimmed = padded_2(slab, (("depth", 2),), 1)
    rimmed = jnp.pad(rimmed, ((0, 0), (0, 0), (0, 0), (1, 1), (1, 1)))
    summed = mix_taps(rimmed, conv_weight, slab_planes, row_count * depth_count, columns)
    return summed.astype(jnp.bfloat16)


def solution(mesh):
    return jax.shard_map(
        on_device,
        mesh=mesh,
        in_specs=(
            P("view", None, None),
            P("view", None),
            P(),
            P("view", None, None, "depth", None),
            P(),
        ),
        out_specs=P("view", None, "depth", None, None),
        check_vma=False,
    )
```

profile of v0, /device:TPU:1, one launch (start us, length us, event | category | flops | bytes accessed | tf_op | source)
XLA Modules:
  0.0 1019.4 jit_solution(8187742426238221678)
XLA Ops:
  6.5 0.7 all-gather.2.cloned.1.call-update
  7.3 0.7 fusion.81
  8.1 0.9 gather_fusion.1
  9.1 0.8 constant_dynamic-slice_fusion.2
  9.9 50.2 %all-gather.2.cloned.1.call-done = bf16[48,1024,32]{1,2,0:T(8,128)(2,1)} async-done(((bf16[3,1024,32]{1,2,0:T(8,128)(2,1)}), bf16[48,1024,32]{1,2,0:T(8,128)(2,1)}) %all-gather.2.cloned.1.call-update) | async-done | bytes 3145744 | tf_op jit(solution)/shard_map/all_gather | solution.py:57
  60.1 11.0 %copy.343 = bf16[48,1024,32]{2,1,0:T(8,128)(2,1)} copy(bf16[48,1024,32]{1,2,0:T(8,128)(2,1)} %all-gather.2.cloned.1.call-done) | data formatting | bytes 6291456 | tf_op jit(solution)/shard_map/while | solution.py:81
  71.1 909.2 %while.10 = (s32[]{:T(128)}, bf16[3,8,64,1,128]{4,1,0,3,2:T(8,128)(2,1)}, s32[3,10,64,1,128]{4,2,1,3,0:T(8,128)S(1)}, bf16[3,128,32]{1,2,0:T(8,128)(2,1)S(1)}, s...) while((s32[]{:T(128)}, bf16[3,8,64,1,128]{4,1,0,3,2:T(8,128)(2,1)}, ...), condition=%wide.region_3.4_spmd, body=%wide.region_0.3_spmd.sunk | while | flops 12587020 | bytes 46916348 | solution.py:81
  71.4 0.5 compare_select_fusion.5
  72.0 278.2 %gather_fusion = bf16[81920,32]{1,0:T(8,128)(2,1)} fusion(bf16[49152,32]{1,0:T(8,128)(2,1)} %get-tuple-element.177, s32[81920]{0:T(1024)S(1)} %broadcast_clamp_fusion.2), kind=kCustom, calls=%fused_computation.clone.1 | custom fusion | bytes 10813440 | tf_op jit(solution)/shard_map/while/body/eval_jaxpr/jit(_take)/gather | solution.py:69
  350.1 17.3 %copy.427 = bf16[81920,32]{0,1:T(8,128)(2,1)} copy(bf16[81920,32]{1,0:T(8,128)(2,1)} %gather_fusion) | data formatting | bytes 10485760 | tf_op jit(solution)/shard_map/while/body/eval_jaxpr/jit(_take)/gather | solution.py:69
  367.5 3.7 copy.428
  371.2 1.6 multiply_reduce_fusion.2
  373.4 0.8 copy_dynamic-update-slice_fusion.2
  374.5 0.5 compare_select_fusion.5
  375.0 278.2 %gather_fusion = bf16[81920,32]{1,0:T(8,128)(2,1)} fusion(bf16[49152,32]{1,0:T(8,128)(2,1)} %get-tuple-element.177, s32[81920]{0:T(1024)S(1)} %broadcast_clamp_fusion.2), kind=kCustom, calls=%fused_computation.clone.1 | custom fusion | bytes 10813440 | tf_op jit(solution)/shard_map/while/body/eval_jaxpr/jit(_take)/gather | solution.py:69
  653.2 17.3 %copy.427 = bf16[81920,32]{0,1:T(8,128)(2,1)} copy(bf16[81920,32]{1,0:T(8,128)(2,1)} %gather_fusion) | data formatting | bytes 10485760 | tf_op jit(solution)/shard_map/while/body/eval_jaxpr/jit(_take)/gather | solution.py:69
  670.5 3.7 copy.428
  674.3 1.6 multiply_reduce_fusion.2
  676.5 0.8 copy_dynamic-update-slice_fusion.2
  677.5 0.5 compare_select_fusion.5
  678.1 278.2 %gather_fusion = bf16[81920,32]{1,0:T(8,128)(2,1)} fusion(bf16[49152,32]{1,0:T(8,128)(2,1)} %get-tuple-element.177, s32[81920]{0:T(1024)S(1)} %broadcast_clamp_fusion.2), kind=kCustom, calls=%fused_computation.clone.1 | custom fusion | bytes 10813440 | tf_op jit(solution)/shard_map/while/body/eval_jaxpr/jit(_take)/gather | solution.py:69
  956.3 17.3 %copy.427 = bf16[81920,32]{0,1:T(8,128)(2,1)} copy(bf16[81920,32]{1,0:T(8,128)(2,1)} %gather_fusion) | data formatting | bytes 10485760 | tf_op jit(solution)/shard_map/while/body/eval_jaxpr/jit(_take)/gather | solution.py:69
  973.6 3.7 copy.428
  977.3 1.6 multiply_reduce_fusion.2
  979.6 0.8 copy_dynamic-update-slice_fusion.2
  980.3 5.5 all-to-all-start
  989.8 3.8 all-to-all-done
  993.7 3.3 collective-permute-start
  997.0 2.1 collective-permute-start.1
  999.4 3.0 collective-permute-done.1
  1002.4 0.5 select_maximum_fusion
  1003.9 0.3 fusion.55
  1004.5 0.3 fusion.59
  1004.8 0.3 fusion.61
  1005.2 0.3 fusion.63
  1005.5 0.3 fusion.65
  1005.8 0.3 fusion.67
  1006.1 0.3 fusion.69
  1006.4 0.3 fusion.71
  1006.8 0.3 convolution_bitcast_fusion.5
  1007.1 0.3 convolution_bitcast_fusion.6
  1009.0 0.3 convolution_add_fusion.3
  1009.3 0.3 convolution_add_fusion.2
  1010.0 0.7 fusion.31
  1010.6 0.4 fusion.13
  1011.0 0.3 fusion.18
  1011.3 0.3 fusion.32
  1011.7 0.8 copy.309
  (91 shorter events, 10.4 us)
Async XLA Ops:
  6.5 1.5 copy-start
  6.5 3.3 copy-start.4
  6.5 53.6 %all-gather.2.cloned.1.call-start = ((), (), s32[]{:S(2)}) async-start(), calls=%async_computation.1 | async-start | bytes 3342336 | tf_op jit(solution)/shard_map/all_gather | solution.py:57
  9.8 61.3 %copy-start.3 = (s32[3,10,64,1,128]{4,3,2,1,0:T(1,128)S(1)}, s32[3,10,64,1,128]{4,3,2,1,0:T(1,128)}, u32[]{:S(2)}) copy-start(s32[3,10,64,1,128]{4,3,2,1,0:T(1,128)} %param.10) | copy-start | bytes 2949124
  71.1 914.7 %copy-start.2 = (bf16[27,8,8]{0,2,1:T(8,128)(2,1)S(1)}, bf16[27,8,8]{0,2,1:T(8,128)(2,1)}, u32[]{:S(2)}) copy-start(bf16[27,8,8]{0,2,1:T(8,128)(2,1)} %param.11) | copy-start | bytes 10372
  980.3 13.2 %all-to-all-start = ((bf16[3,8,64,1,128]{4,1,0,3,2:T(8,128)(2,1)}), bf16[3,8,64,1,128]{4,1,0,3,2:T(8,128)(2,1)S(1)}, u32[]{:S(2)}, u32[]{:S(2)}) async-start(bf16[3,8,64,1,128]{4,1,0,3,2:T(8,128)(2,1)} %get-tuple-element.37), calls=%async_computation | async-start | bytes 786432 | tf_op jit(solution)/shard_map/all_to_all | solution.py:83
  993.7 5.7 collective-permute-start
  997.0 5.4 collective-permute-start.1
  1011.0 1.5 copy-start.1
Sparse Core Ops, SparseCore 0:
  9.5 50.5 all-gather.1
where the time goes:
time: 1020 us
  local copies, waits for them, and re-layouts  918 us (90%)
  waiting for transfers between devices  57.7 us (6%)
  between operations  13.7 us (1%)
  starting transfers between devices  10.9 us (1%)
    gather x6, local copies, waits for them, and re-layouts, one_view(): warped = jnp.take(flat_pool, picks.reshape(-1), axis=0)  886 us
    all_gather x1, waiting for transfers between devices, on_device(): tile_pool = lax.all_gather(features, 'view', axis=0, tiled=True)  50.2 us
  transfers between devices with their start and end apart: 4, of which 3 were waited for; matrix products, arithmetic and copies ran while one was open for 1% of the time, Pallas kernels for 0%

commit v1 on v0

v1 whole, which is shorter than its diff:
```python
import functools

import jax
import jax.numpy as jnp
from jax import lax
from jax.experimental import pallas as pl
from jax.experimental.pallas import tpu as pltpu
from jax.sharding import PartitionSpec as P

LOW = 256


def cost_kernel(source_ref, here_ref, warp_ref, own_ref, pool_ref, out_ref, low_ref, high_ref, scale_ref, sums_ref):
    view = pl.program_id(0)
    sources, planes, columns = warp_ref.shape[1:]
    channels = own_ref.shape[1]
    slabs = out_ref.shape[0]
    groups = out_ref.shape[3]
    slab = planes // slabs
    block = 4
    warp = warp_ref[0]
    outside = warp < 0
    low_ref[...] = jnp.where(outside, -1, warp & (LOW - 1)).astype(jnp.float32)
    high_ref[...] = warp >> 8
    live = jnp.sum(jnp.where(outside, 0.0, 1.0), axis=0)
    scale_ref[...] = 0.5 / jnp.maximum(live, 1.0)
    tiles = LOW // 16
    pixel = lax.broadcasted_iota(jnp.int32, (tiles, 16, columns), 0) * 16 + lax.broadcasted_iota(
        jnp.int32, (tiles, 16, columns), 1
    )
    pixel = pixel.astype(jnp.float32).astype(jnp.bfloat16)
    one = jnp.ones((), jnp.bfloat16)
    zero = jnp.zeros((), jnp.bfloat16)
    own = own_ref[0].astype(jnp.float32)

    def planes_of(start):
        totals = [jnp.zeros((channels, columns), jnp.float32) for _ in range(block)]
        for s in range(sources):
            tile = pool_ref[source_ref[view, s]]
            lhs = jnp.concatenate([tile[:, h * LOW : (h + 1) * LOW] for h in range(4)], axis=0)
            hots = []
            for j in range(block):
                row = jnp.broadcast_to(low_ref[s, pl.ds(start + j, 1), :], (16, columns)).astype(jnp.bfloat16)
                hots.append(jnp.where(pixel == row[None], one, zero).reshape(LOW, columns))
            picked = jnp.dot(lhs, jnp.concatenate(hots, axis=1), preferred_element_type=jnp.float32)
            for j in range(block):
                high = jnp.broadcast_to(high_ref[s, pl.ds(start + j, 1), :], (channels, columns))
                odd = (high & 1) == 1
                upper = (high & 2) == 2
                part = picked[:, j * columns : (j + 1) * columns]
                q = [part[h * channels : (h + 1) * channels] for h in range(4)]
                totals[j] = totals[j] + jnp.where(upper, jnp.where(odd, q[3], q[2]), jnp.where(odd, q[1], q[0]))
        costs = []
        for j in range(block):
            sums_ref[j] = totals[j] * own
            size = channels // groups
            corr = sums_ref[j, pl.ds(0, groups, stride=size), :]
            for n in range(1, size):
                corr = corr + sums_ref[j, pl.ds(n, groups, stride=size), :]
            corr = corr * jnp.broadcast_to(scale_ref[pl.ds(start + j, 1), :], (groups, columns))
            costs.append(corr.astype(jnp.bfloat16))
        return costs

    out_ref[0, 0, 0] = jnp.zeros((groups, columns), jnp.bfloat16)
    out_ref[slabs - 1, 0, slab + 1] = jnp.zeros((groups, columns), jnp.bfloat16)

    def step(half, carry):
        t = half // 2
        inner = (half % 2) * block
        costs = planes_of(half * block)
        for j in range(block):
            out_ref[t, 0, 1 + inner + j] = costs[j]

        @pl.when((inner == 0) & (t > 0))
        def _():
            out_ref[t - 1, 0, slab + 1] = costs[0]

        @pl.when((inner > 0) & (t < slabs - 1))
        def _():
            out_ref[t + 1, 0, 0] = costs[block - 1]

        return carry

    lax.fori_loop(0, planes // block, step, 0)


def cost_slabs(source_ids, here, warp, tiles, pool, slabs, groups):
    views, sources, planes, columns = warp.shape
    channels = tiles.shape[1]
    slab = planes // slabs
    return pl.pallas_call(
        cost_kernel,
        grid_spec=pltpu.PrefetchScalarGridSpec(
            num_scalar_prefetch=2,
            grid=(views,),
            in_specs=[
                pl.BlockSpec((1, sources, planes, columns), lambda v, s, h: (v, 0, 0, 0)),
                pl.BlockSpec((1, channels, columns), lambda v, s, h: (v, 0, h[0])),
                pl.BlockSpec(pool.shape, lambda v, s, h: (0, 0, 0), pipeline_mode=pl.Buffered(1)),
            ],
            out_specs=pl.BlockSpec((slabs, 1, slab + 2, groups, columns), lambda v, s, h: (0, v, 0, 0, 0)),
            scratch_shapes=[
                pltpu.VMEM((sources, planes, columns), jnp.float32),
                pltpu.VMEM((sources, planes, columns), jnp.int32),
                pltpu.VMEM((planes, columns), jnp.float32),
                pltpu.VMEM((4, channels, columns), jnp.float32),
            ],
        ),
        out_shape=jax.ShapeDtypeStruct((slabs, views, slab + 2, groups, columns), jnp.bfloat16),
        name="cost",
    )(source_ids, here, warp, tiles, pool)


def mix_kernel(weight_ref, slab_ref, out_ref, rows_ref):
    rows, _, padded, groups, columns = slab_ref.shape
    planes = padded - 2
    lane = lax.broadcasted_iota(jnp.int32, (groups, columns), 1)
    blank = jnp.zeros((groups, columns), jnp.float32)
    empty = jnp.zeros((4 * groups, columns), jnp.bfloat16)
    weight = weight_ref[...]
    terms = []
    for d in range(padded):
        taps = []
        for i in range(rows):
            cell = slab_ref[i, 0, d].astype(jnp.float32)
            left = jnp.where(lane == 0, 0.0, pltpu.roll(cell, 1, 1))
            right = jnp.where(lane == columns - 1, 0.0, pltpu.roll(cell, columns - 1, 1))
            taps.append(jnp.concatenate([left, cell, right, blank], axis=0).astype(jnp.bfloat16))
        above = jnp.concatenate([empty] + taps[:-1], axis=1)
        below = jnp.concatenate(taps[1:] + [empty], axis=1)
        matrix = jnp.concatenate([above, jnp.concatenate(taps, axis=1), below], axis=0)
        terms.append(jnp.dot(weight, matrix, preferred_element_type=jnp.float32))
        if d >= 2:
            mixed = terms[d - 2][0:groups] + terms[d - 1][groups : 2 * groups] + terms[d][2 * groups : 3 * groups]
            for i in range(rows):
                rows_ref[pl.ds(i, groups, stride=rows), :] = mixed[:, i * columns : (i + 1) * columns]
            for h in range(groups):
                out_ref[0, h, d - 2] = rows_ref[h * rows : (h + 1) * rows, :].astype(jnp.bfloat16)


def mix_slabs(weight, slabs):
    rows, views, padded, groups, columns = slabs.shape
    return pl.pallas_call(
        mix_kernel,
        grid=(views,),
        in_specs=[
            pl.BlockSpec(weight.shape, lambda v: (0, 0)),
            pl.BlockSpec((rows, 1, padded, groups, columns), lambda v: (0, v, 0, 0, 0)),
        ],
        out_specs=pl.BlockSpec((1, groups, padded - 2, rows, columns), lambda v: (v, 0, 0, 0, 0)),
        out_shape=jax.ShapeDtypeStruct((views, groups, padded - 2, rows, columns), jnp.bfloat16),
        scratch_shapes=[pltpu.VMEM((groups * rows, columns), jnp.float32)],
        name="mix",
    )(weight, slabs)


def on_device(features, view_lists, requests, warp_idx, conv_weight):
    view_here = lax.axis_index("view")
    depth_here = lax.axis_index("depth")
    depth_count = lax.axis_size("depth")
    local_views = features.shape[0]
    groups = conv_weight.shape[1]
    asked = requests.shape[2]
    tiles = jnp.transpose(features, (0, 2, 1))
    pool = lax.all_gather(tiles, "view", axis=0, tiled=True)
    owner_dev = view_lists // asked
    slot_index = view_lists % asked
    source_ids = owner_dev * local_views + requests[view_here, owner_dev, slot_index]
    warp = warp_idx.reshape(warp_idx.shape[:3] + warp_idx.shape[4:])
    slabs = cost_slabs(source_ids, depth_here.reshape(1), warp, tiles, pool, depth_count, groups)
    slabs = lax.all_to_all(slabs, "depth", split_axis=0, concat_axis=0, tiled=True)
    taps = conv_weight.reshape(3, 3, 3 * groups, groups)
    taps = jnp.pad(taps, ((0, 0), (0, 0), (0, groups), (0, 0)))
    weight = jnp.transpose(taps, (0, 3, 1, 2)).reshape(3 * groups, 12 * groups)
    return mix_slabs(weight, slabs)


def solution(mesh):
    return jax.shard_map(
        on_device,
        mesh=mesh,
        in_specs=(
            P("view", None, None),
            P("view", None),
            P(),
            P("view", None, None, "depth", None),
            P(),
        ),
        out_specs=P("view", None, "depth", None, None),
        check_vma=False,
    )
```

time: 1020 us -> 116 us (0.11)
  local copies, waits for them, and re-layouts: 918 us -> 2.83 us
  Pallas kernels: 0 us -> 33.8 us
    gather x6 -> x0, local copies, waits for them, and re-layouts: 886 us -> none  [one_view(): warped = jnp.take(flat_pool, picks.reshape(-1), axis=0)]
    pallas_call x0 -> x2, Pallas kernels: none -> 33.8 us  [the longest x1 30.3 us: cost_slabs(): pl.pallas_call(cost_kernel, grid_spec=pltpu.PrefetchScalarGridSpec(num_sc...]
    while x4 -> x0, local copies, waits for them, and re-layouts: 22.2 us -> none
  transfers between devices with their start and end apart: 4 -> 2, of which waited for: 3 -> 2; matrix products, arithmetic and copies ran while one was open for 1% -> 3% of each run, Pallas kernels for 0% -> 0%
where the time goes in v1:
time: 116 us
  waiting for transfers between devices  58.5 us (50%)
  Pallas kernels  33.8 us (29%)
  between operations  13.4 us (12%)
  starting transfers between devices  5.55 us (5%)
  local copies, waits for them, and re-layouts  2.83 us (2%)
  other arithmetic  1.98 us (2%)
    all_gather x1, waiting for transfers between devices, on_device(): pool = lax.all_gather(tiles, 'view', axis=0, tiled=True)  49.8 us
    pallas_call x1, Pallas kernels, cost_slabs(): pl.pallas_call(cost_kernel, grid_spec=pltpu.PrefetchScalarGridSpec(num_sc...  30.3 us
    all_to_all x1, waiting for transfers between devices, on_device(): lax.all_to_all(slabs, 'depth', split_axis=0, concat_axis=0, tiled=True)  8 us
    all_to_all x1, starting transfers between devices, on_device(): lax.all_to_all(slabs, 'depth', split_axis=0, concat_axis=0, tiled=True)  5.55 us
    pallas_call x1, Pallas kernels, mix_slabs(): pl.pallas_call(mix_kernel, grid=(views,), in_specs=[pl.BlockSpec(weight.s...  3.51 us
  transfers between devices with their start and end apart: 2, of which 2 were waited for; matrix products, arithmetic and copies ran while one was open for 3% of the time, Pallas kernels for 0%

profile of v1, /device:TPU:1, one launch (start us, length us, event | category | flops | bytes accessed | tf_op | source)
XLA Modules:
  0.0 116.1 jit_solution(17946690921313506796)
XLA Ops:
  6.5 0.0 copy-start
  6.5 0.0 all-gather.2.cloned.1.call-start
  6.5 0.7 all-gather.2.cloned.1.call-update
  7.3 0.7 fusion.3
  8.0 0.1 reshape.16
  8.1 0.0 copy-done
  8.1 0.9 gather_fusion
  9.0 0.0 copy-start.2
  9.0 0.1 reshape.19
  9.1 1.3 %multiply_add_fusion.source_ref = s32[3,10]{1,0:T(4,128)} fusion(s32[3,10]{1,0:T(4,128)S(1)} %reshape.19, s32[3,10]{1,0:T(4,128)} %param.6), kind=kLoop, calls=%fused_computation.15 | loop fusion | flops 510 | bytes 360 | tf_op jit(solution)/shard_map/add | solution.py:168
  10.3 49.8 %all-gather.2.cloned.1.call-done.pool_ref = bf16[48,32,1024]{2,1,0:T(8,128)(2,1)} async-done(((bf16[3,32,1024]{2,1,0:T(8,128)(2,1)}), bf16[48,32,1024]{2,1,0:T(8,128)(2,1)}) %all-gather.2.cloned.1.call-update) | async-done | bytes 3145744 | tf_op jit(solution)/shard_map/all_gather | solution.py:165
  60.1 30.3 %cost.1 = bf16[8,3,10,8,128]{4,3,2,1,0:T(8,128)(2,1)} custom-call(s32[3,10]{1,0:T(4,128)} %multiply_add_fusion.source_ref, s32[1]{0:T(128)} %bitcast.1.here_ref, s32[3,10,64,128]{3,2,1,0:T(8,128)} %bitcast.7, bf16[3,32,1024]{2,1,0:T(8,128)(2,1)} %bitcast.9, bf16[48,32,1024]{2,1,0:T(8,128)(2,1)} %all-gather.2.cloned.1.call-done.pool_ref), custom_call_target="tpu_custom_call" | custom-call | tf_op jit(solution)/shard_map/cost/pallas_call | solution.py:91
  90.4 5.5 %all-to-all-start = ((bf16[8,3,10,8,128]{4,3,2,1,0:T(8,128)(2,1)}), bf16[8,3,10,8,128]{4,3,2,1,0:T(8,128)(2,1)S(1)}, u32[]{:S(2)}, u32[]{:S(2)}) async-start(bf16[8,3,10,8,128]{4,3,2,1,0:T(8,128)(2,1)} %cost.1), calls=%async_computation | async-start | bytes 983040 | tf_op jit(solution)/shard_map/all_to_all | solution.py:171
  96.0 0.0 copy-done.2
  96.0 0.1 copy.8
  96.1 0.1 reshape.12
  96.3 0.7 reshape.13.weight_ref
  97.0 8.0 %all-to-all-done.slab_ref = bf16[8,3,10,8,128]{4,3,2,1,0:T(8,128)(2,1)S(1)} async-done(((bf16[8,3,10,8,128]{4,3,2,1,0:T(8,128)(2,1)}), bf16[8,3,10,8,128]{4,3,2,1,0:T(8,128)(2,1)S(1)}, u32[]{:S(2)}, u32[]{:S(2)}) %all-to-all-start) | async-done | bytes 491552 | tf_op jit(solution)/shard_map/all_to_all | solution.py:171
  105.0 0.0 copy-start.1
  105.0 0.8 copy-done.1
  105.7 3.5 %mix.1 = bf16[3,8,8,8,128]{4,3,2,1,0:T(8,128)(2,1)} custom-call(bf16[24,96]{1,0:T(8,128)(2,1)} %reshape.13.weight_ref, bf16[8,3,10,8,128]{4,3,2,1,0:T(8,128)(2,1)} %copy-done.1), custom_call_target="tpu_custom_call" | custom-call | tf_op jit(solution)/shard_map/mix/pallas_call | solution.py:143
  (2 shorter events, 0.0 us)
Async XLA Ops:
  6.5 1.5 %copy-start = (s32[16,16,2]{1,2,0:T(2,128)S(1)}, s32[16,16,2]{1,2,0:T(2,128)}, u32[]{:S(2)}) copy-start(s32[16,16,2]{1,2,0:T(2,128)} %param.7) | copy-start | bytes 6148
  6.5 53.6 %all-gather.2.cloned.1.call-start = ((), (), s32[]{:S(2)}) async-start(), calls=%async_computation.1 | async-start | bytes 3342336 | tf_op jit(solution)/shard_map/all_gather | solution.py:165
  9.0 87.0 %copy-start.2 = (bf16[27,8,8]{0,2,1:T(8,128)(2,1)S(1)}, bf16[27,8,8]{0,2,1:T(8,128)(2,1)}, u32[]{:S(2)}) copy-start(bf16[27,8,8]{0,2,1:T(8,128)(2,1)} %param.9) | copy-start | bytes 10372
  90.4 14.5 %all-to-all-start = ((bf16[8,3,10,8,128]{4,3,2,1,0:T(8,128)(2,1)}), bf16[8,3,10,8,128]{4,3,2,1,0:T(8,128)(2,1)S(1)}, u32[]{:S(2)}, u32[]{:S(2)}) async-start(bf16[8,3,10,8,128]{4,3,2,1,0:T(8,128)(2,1)} %cost.1), calls=%async_computation | async-start | bytes 983040 | tf_op jit(solution)/shard_map/all_to_all | solution.py:171
  105.0 0.8 copy-start.1
Sparse Core Ops, SparseCore 0:
  9.5 50.5 all-gather.1

commit v2 on v1

v2 whole, which is shorter than its diff:
```python
import functools

import jax
import jax.numpy as jnp
from jax import lax
from jax.experimental import pallas as pl
from jax.experimental.pallas import tpu as pltpu
from jax.sharding import PartitionSpec as P

LOW = 256
BLOCK = 4


def ask_kernel(requests_ref, tiles_ref, out_ref):
    here = lax.axis_index("view")
    half = out_ref.shape[3]
    start = pl.multiple_of((lax.axis_index("depth") % 2) * half, half)
    for u in range(out_ref.shape[0]):
        for c in range(out_ref.shape[1]):
            out_ref[u, c] = tiles_ref[requests_ref[u, c, here], :, pl.ds(start, half)]


def asked_tiles(requests, tiles):
    askers, slots, _ = requests.shape
    _, channels, pixels = tiles.shape
    return pl.pallas_call(
        ask_kernel,
        in_specs=[pl.BlockSpec(memory_space=pltpu.SMEM), pl.BlockSpec(memory_space=pltpu.VMEM)],
        out_specs=pl.BlockSpec(memory_space=pltpu.VMEM),
        out_shape=jax.ShapeDtypeStruct((askers, slots, channels, pixels // 2), jnp.bfloat16),
        name="ask",
    )(requests, tiles)


def pack_kernel(warp_ref, out_ref):
    slabs, views, sources, slab, _ = out_ref.shape
    for v in range(views):
        for s in range(sources):
            for t in range(slabs):
                out_ref[t, v, s] = warp_ref[v, s, t * slab : (t + 1) * slab].astype(jnp.int16)


def packed_warp(warp, slabs):
    views, sources, planes, columns = warp.shape
    return pl.pallas_call(
        pack_kernel,
        in_specs=[pl.BlockSpec(memory_space=pltpu.VMEM)],
        out_specs=pl.BlockSpec(memory_space=pltpu.VMEM),
        out_shape=jax.ShapeDtypeStruct((slabs, views, sources, planes // slabs, columns), jnp.int16),
        cost_estimate=pl.CostEstimate(flops=warp.size, bytes_accessed=warp.size * 6, transcendentals=0),
        name="pack",
    )(warp)


def cost_kernel(slot_ref, warp_ref, own_ref, near_ref, far_ref, out_ref, low_ref, high_ref, scale_ref, sums_ref, *, chosen):
    view = pl.program_id(0)
    rows, _, sources, _, columns = warp_ref.shape
    channels = own_ref.shape[1]
    groups = out_ref.shape[3]
    size = channels // groups
    count = len(chosen)
    flip = (lax.axis_index("depth") % 2) * 2
    for i in range(rows):
        live = jnp.zeros((warp_ref.shape[3], columns), jnp.float32)
        for s in range(sources):
            warp = warp_ref[i, 0, s].astype(jnp.int32)
            outside = warp < 0
            low_ref[s, i] = jnp.where(outside, -1, warp & (LOW - 1)).astype(jnp.float32)
            high_ref[s, i] = (warp >> 8) ^ flip
            live = live + jnp.where(outside, 0.0, 1.0)
        scale_ref[i] = 0.5 / jnp.maximum(live, 1.0)
    tiles = LOW // 16
    pixel = lax.broadcasted_iota(jnp.int32, (tiles, 16, columns), 0) * 16 + lax.broadcasted_iota(
        jnp.int32, (tiles, 16, columns), 1
    )
    pixel = pixel.astype(jnp.float32).astype(jnp.bfloat16)
    one = jnp.ones((), jnp.bfloat16)
    zero = jnp.zeros((), jnp.bfloat16)

    def cells_of(cells):
        totals = [jnp.zeros((channels, columns), jnp.float32) for _ in cells]
        for s in range(sources):
            slot = slot_ref[view, s]
            near = near_ref[slot]
            far = far_ref[slot]
            lhs = jnp.concatenate([near[:, :LOW], near[:, LOW:], far[:, :LOW], far[:, LOW:]], axis=0)
            hots = []
            for i, d in cells:
                row = jnp.broadcast_to(low_ref[s, i, pl.ds(d, 1), :], (16, columns)).astype(jnp.bfloat16)
                hots.append(jnp.where(pixel == row[None], one, zero).reshape(LOW, columns))
            picked = jnp.dot(lhs, jnp.concatenate(hots, axis=1), preferred_element_type=jnp.float32)
            for j, (i, d) in enumerate(cells):
                high = jnp.broadcast_to(high_ref[s, i, pl.ds(d, 1), :], (channels, columns))
                odd = (high & 1) == 1
                upper = (high & 2) == 2
                part = picked[:, j * columns : (j + 1) * columns]
                q = [part[h * channels : (h + 1) * channels] for h in range(4)]
                totals[j] = totals[j] + jnp.where(upper, jnp.where(odd, q[3], q[2]), jnp.where(odd, q[1], q[0]))
        for j, (i, d) in enumerate(cells):
            own = own_ref[0, :, pl.ds(pl.multiple_of(i * columns, columns), columns)].astype(jnp.float32)
            sums_ref[j] = totals[j] * own
            corr = sums_ref[j, pl.ds(0, groups, stride=size), :]
            for n in range(1, size):
                corr = corr + sums_ref[j, pl.ds(n, groups, stride=size), :]
            corr = corr * jnp.broadcast_to(scale_ref[i, pl.ds(d, 1), :], (groups, columns))
            out_ref[0, chosen.index(d), i] = corr.astype(jnp.bfloat16)

    pair = [(r, d) for r in range(2) for d in chosen]

    def step(half, carry):
        for b in range(0, len(pair), BLOCK):
            cells_of([(2 * half + r, d) for r, d in pair[b : b + BLOCK]])
        return carry

    lax.fori_loop(0, rows // 2, step, 0)


def costs(slots, warp, tiles, near, far, groups, chosen):
    rows, views, sources, planes, columns = warp.shape
    channels = tiles.shape[1]
    count = len(chosen)
    work = count * views * rows * sources * columns
    return pl.pallas_call(
        functools.partial(cost_kernel, chosen=chosen),
        grid_spec=pltpu.PrefetchScalarGridSpec(
            num_scalar_prefetch=1,
            grid=(views,),
            in_specs=[
                pl.BlockSpec((rows, 1, sources, planes, columns), lambda v, s: (0, v, 0, 0, 0)),
                pl.BlockSpec((1, channels, tiles.shape[2]), lambda v, s: (v, 0, 0)),
                pl.BlockSpec(near.shape, lambda v, s: (0, 0, 0), pipeline_mode=pl.Buffered(1)),
                pl.BlockSpec(far.shape, lambda v, s: (0, 0, 0), pipeline_mode=pl.Buffered(1)),
            ],
            out_specs=pl.BlockSpec((1, count, rows, groups, columns), lambda v, s: (v, 0, 0, 0, 0)),
            scratch_shapes=[
                pltpu.VMEM((sources, rows, planes, columns), jnp.float32),
                pltpu.VMEM((sources, rows, planes, columns), jnp.int32),
                pltpu.VMEM((rows, planes, columns), jnp.float32),
                pltpu.VMEM((BLOCK, channels, columns), jnp.float32),
            ],
        ),
        out_shape=jax.ShapeDtypeStruct((views, count, rows, groups, columns), jnp.bfloat16),
        cost_estimate=pl.CostEstimate(flops=work * 2 * 128 * LOW, bytes_accessed=near.size * 4, transcendentals=0),
        name="cost",
    )(slots, warp, tiles, near, far)


def mix_kernel(weight_ref, before_ref, edge_ref, inner_ref, after_ref, out_ref, rows_ref):
    _, inside, rows, groups, columns = inner_ref.shape
    padded = inside + 4
    lane = lax.broadcasted_iota(jnp.int32, (groups, columns), 1)
    blank = jnp.zeros((groups, columns), jnp.float32)
    empty = jnp.zeros((4 * groups, columns), jnp.bfloat16)
    weight = weight_ref[...]
    terms = []
    for d in range(padded):
        taps = []
        for i in range(rows):
            if d == 0:
                cell = before_ref[0, 0, i]
            elif d == padded - 1:
                cell = after_ref[0, 0, i]
            elif d == 1:
                cell = edge_ref[0, 0, i]
            elif d == padded - 2:
                cell = edge_ref[0, 1, i]
            else:
                cell = inner_ref[0, d - 2, i]
            cell = cell.astype(jnp.float32)
            left = jnp.where(lane == 0, 0.0, pltpu.roll(cell, 1, 1))
            right = jnp.where(lane == columns - 1, 0.0, pltpu.roll(cell, columns - 1, 1))
            taps.append(jnp.concatenate([left, cell, right, blank], axis=0).astype(jnp.bfloat16))
        above = jnp.concatenate([empty] + taps[:-1], axis=1)
        below = jnp.concatenate(taps[1:] + [empty], axis=1)
        matrix = jnp.concatenate([above, jnp.concatenate(taps, axis=1), below], axis=0)
        terms.append(jnp.dot(weight, matrix, preferred_element_type=jnp.float32))
        if d >= 2:
            mixed = terms[d - 2][0:groups] + terms[d - 1][groups : 2 * groups] + terms[d][2 * groups : 3 * groups]
            for i in range(rows):
                rows_ref[pl.ds(i, groups, stride=rows), :] = mixed[:, i * columns : (i + 1) * columns]
            for h in range(groups):
                out_ref[0, h, d - 2] = rows_ref[h * rows : (h + 1) * rows, :].astype(jnp.bfloat16)


def mixed(weight, before, edge, inner, after):
    views, inside, rows, groups, columns = inner.shape

    def part(planes):
        return pl.BlockSpec((1, planes, rows, groups, columns), lambda v: (v, 0, 0, 0, 0))

    return pl.pallas_call(
        mix_kernel,
        grid=(views,),
        in_specs=[pl.BlockSpec(weight.shape, lambda v: (0, 0)), part(1), part(2), part(inside), part(1)],
        out_specs=pl.BlockSpec((1, groups, inside + 2, rows, columns), lambda v: (v, 0, 0, 0, 0)),
        out_shape=jax.ShapeDtypeStruct((views, groups, inside + 2, rows, columns), jnp.bfloat16),
        scratch_shapes=[pltpu.VMEM((groups * rows, columns), jnp.float32)],
        name="mix",
    )(weight, before, edge, inner, after)


def on_device(features, view_lists, requests, warp_idx, conv_weight):
    slabs = lax.axis_size("depth")
    groups = conv_weight.shape[1]
    tiles = jnp.transpose(features, (0, 2, 1))
    channels = tiles.shape[1]
    half = tiles.shape[2] // 2
    send = asked_tiles(jnp.transpose(requests, (0, 2, 1)), tiles)
    near = lax.all_to_all(send, "view", split_axis=0, concat_axis=0, tiled=True)
    near = near.reshape(-1, channels, half)
    far = lax.ppermute(near, "depth", [(i, i ^ 1) for i in range(slabs)])
    warp = packed_warp(warp_idx.reshape(warp_idx.shape[:3] + warp_idx.shape[4:]), slabs)
    warp = lax.all_to_all(warp, "depth", split_axis=0, concat_axis=0, tiled=True)
    planes = warp.shape[3]
    edge = costs(view_lists, warp, tiles, near, far, groups, (0, planes - 1))
    before = lax.ppermute(edge[:, 1:], "depth", [(i, i + 1) for i in range(slabs - 1)])
    after = lax.ppermute(edge[:, :1], "depth", [(i + 1, i) for i in range(slabs - 1)])
    inner = costs(view_lists, warp, tiles, near, far, groups, tuple(range(1, planes - 1)))
    taps = conv_weight.reshape(3, 3, 3 * groups, groups)
    taps = jnp.pad(taps, ((0, 0), (0, 0), (0, groups), (0, 0)))
    weight = jnp.transpose(taps, (0, 3, 1, 2)).reshape(3 * groups, 12 * groups)
    return mixed(weight, before, edge, inner, after)


def solution(mesh):
    return jax.shard_map(
        on_device,
        mesh=mesh,
        in_specs=(
            P("view", None, None),
            P("view", None),
            P(),
            P("view", None, None, "depth", None),
            P(),
        ),
        out_specs=P("view", None, "depth", None, None),
        check_vma=False,
    )
```

time: 116 us -> 86.6 us (0.75)
  waiting for transfers between devices: 58.5 us -> 8 us
  blocking collectives: 0 us -> 24.5 us
  between operations: 13.4 us -> 0.06 us
  starting transfers between devices: 5.55 us -> 12.2 us
  Pallas kernels: 33.8 us -> 36.3 us
  local copies, waits for them, and re-layouts: 2.83 us -> 4.82 us
  other arithmetic: 1.98 us -> 0 us
    all_gather x1 -> x0, waiting for transfers between devices: 49.8 us -> none  [on_device(): pool = lax.all_gather(tiles, 'view', axis=0, tiled=True)]
    all_to_all x0 -> x1, blocking collectives: none -> 24.5 us  [on_device(): near = lax.all_to_all(send, 'view', split_axis=0, concat_axis=0, tiled=True)]
    ppermute x0 -> x3, starting transfers between devices: none -> 7.42 us  [the longest x1 2.86 us: on_device(): lax.ppermute(edge[:, :1], 'depth', [(i + 1, i) for i in range(slabs - 1)])]
    pallas_call x2 -> x5, Pallas kernels: 33.8 us -> 36.3 us  [the longest x2 28.7 us: costs(): pl.pallas_call(functools.partial(cost_kernel, chosen=chosen), grid_spec=p...]
    unnamed x7 -> x13, local copies, waits for them, and re-layouts: 0.92 us -> 3.15 us
    add x1 -> x0, other arithmetic: 1.28 us -> none  [on_device(): owner_dev * local_views + requests[view_here, owner_dev, slot_index]]
  transfers between devices with their start and end apart: 2 -> 4, of which waited for: 2 -> 1; matrix products, arithmetic and copies ran while one was open for 3% -> 1% of each run, Pallas kernels for 0% -> 24%
where the time goes in v2:
time: 86.6 us; the launch traced here: 85.9 us
  Pallas kernels  36.3 us (42%)
  blocking collectives  24.5 us (28%)
  starting transfers between devices  12.2 us (14%)
  waiting for transfers between devices  8 us (9%)
  local copies, waits for them, and re-layouts  4.82 us (6%)
    pallas_call x2, Pallas kernels, costs(): pl.pallas_call(functools.partial(cost_kernel, chosen=chosen), grid_spec=p...  28.7 us
    all_to_all x1, blocking collectives, on_device(): near = lax.all_to_all(send, 'view', split_axis=0, concat_axis=0, tiled=True)  24.5 us
    all_to_all x1, waiting for transfers between devices, on_device(): lax.all_to_all(warp, 'depth', split_axis=0, concat_axis=0, tiled=True)  7.99 us
    all_to_all x1, starting transfers between devices, on_device(): lax.all_to_all(warp, 'depth', split_axis=0, concat_axis=0, tiled=True)  4.81 us
    pallas_call x1, Pallas kernels, mixed(): pl.pallas_call(mix_kernel, grid=(views,), in_specs=[pl.BlockSpec(weight.s...  3.54 us
    unnamed x13, local copies, waits for them, and re-layouts  3.15 us
    ppermute x1, starting transfers between devices, on_device(): lax.ppermute(edge[:, :1], 'depth', [(i + 1, i) for i in range(slabs - 1)])  2.86 us
    ppermute x1, starting transfers between devices, on_device(): lax.ppermute(edge[:, 1:], 'depth', [(i, i + 1) for i in range(slabs - 1)])  2.69 us
  transfers between devices with their start and end apart: 4, of which 1 were waited for; matrix products, arithmetic and copies ran while one was open for 1% of the time, Pallas kernels for 24%

profile of v2, /device:TPU:1, one launch (start us, length us, event | category | flops | bytes accessed | tf_op | source)
XLA Modules:
  0.0 85.9 jit_solution(12760502264048211826)
XLA Ops:
  0.0 2.0 %ask.1 = bf16[16,2,32,512]{3,2,1,0:T(8,128)(2,1)} custom-call(s32[16,2,16]{2,1,0:T(2,128)} %bitcast.15, bf16[3,32,1024]{2,1,0:T(8,128)(2,1)} %bitcast.12), custom_call_target="tpu_custom_call" | custom-call | tf_op jit(solution)/shard_map/ask/pallas_call | solution.py:26
  2.0 24.5 %all_to_all.10 = bf16[16,2,32,512]{3,2,1,0:T(8,128)(2,1)S(1)} all-to-all(bf16[16,2,32,512]{3,2,1,0:T(8,128)(2,1)} %ask.1), channel_id=1, replica_groups=mesh['view'=16,'depth'=8] {'view'}, dimensions={0} | all-to-all | bytes 2097152 | tf_op jit(solution)/shard_map/all_to_all | solution.py:209
  26.5 0.0 copy-start
  26.5 1.9 %collective-permute-start = (bf16[32,32,512]{2,1,0:T(8,128)(2,1)S(1)}, bf16[32,32,512]{2,1,0:T(8,128)(2,1)S(1)}, u32[]{:S(2)}, u32[]{:S(2)}) collective-permute-start(bf16[32,32,512]{2,1,0:T(8,128)(2,1)S(1)} %bitcast.8), channel_id=1, source_target_pairs={{0,1},{1,0},{2,3},{3,2},{4,5},{5,4},{6,7},{7,6},{8,9},{9,8},{10,11... | collective-permute-start | bytes 3145736 | tf_op jit(solution)/shard_map/ppermute | solution.py:211
  28.4 2.1 %pack.1 = s16[8,3,10,8,128]{4,3,2,1,0:T(8,128)(2,1)} custom-call(s32[3,10,64,128]{3,2,1,0:T(8,128)} %bitcast.11), custom_call_target="tpu_custom_call" | custom-call | flops 245760 | bytes 1474560 | tf_op jit(solution)/shard_map/pack/pallas_call | solution.py:45
  30.4 0.0 copy-start.4
  30.4 0.0 copy-done
  30.4 4.8 %all-to-all-start = ((s16[8,3,10,8,128]{4,3,2,1,0:T(8,128)(2,1)}), s16[8,3,10,8,128]{4,3,2,1,0:T(8,128)(2,1)S(1)}, u32[]{:S(2)}, u32[]{:S(2)}) async-start(s16[8,3,10,8,128]{4,3,2,1,0:T(8,128)(2,1)} %pack.1), calls=%async_computation | async-start | bytes 983040 | tf_op jit(solution)/shard_map/all_to_all | solution.py:213
  35.3 0.0 copy-done.4
  35.3 0.1 copy.6
  35.4 0.1 reshape.12
  35.6 0.7 reshape.13.weight_ref
  36.3 8.0 %all-to-all-done.warp_ref = s16[8,3,10,8,128]{4,3,2,1,0:T(8,128)(2,1)S(1)} async-done(((s16[8,3,10,8,128]{4,3,2,1,0:T(8,128)(2,1)}), s16[8,3,10,8,128]{4,3,2,1,0:T(8,128)(2,1)S(1)}, u32[]{:S(2)}, u32[]{:S(2)}) %all-to-all-start) | async-done | bytes 491552 | tf_op jit(solution)/shard_map/all_to_all | solution.py:213
  44.3 0.0 copy-start.1
  44.3 0.0 collective-permute-done.far_ref
  44.3 0.8 copy-done.1
  45.0 0.0 copy-start.5
  45.0 1.0 %copy-done.5 = bf16[32,32,512]{2,1,0:T(8,128)(2,1)} copy-done((bf16[32,32,512]{2,1,0:T(8,128)(2,1)}, bf16[32,32,512]{2,1,0:T(8,128)(2,1)S(1)}, u32[]{:S(2)}) %copy-start.5) | copy-done | bytes 1048600
  46.0 10.0 %cost.2.edge_ref = bf16[3,2,8,8,128]{4,3,2,1,0:T(8,128)(2,1)} custom-call(s32[3,10]{1,0:T(4,128)} %slot_ref.3, s16[8,3,10,8,128]{4,3,2,1,0:T(8,128)(2,1)} %copy-done.1, bf16[3,32,1024]{2,1,0:T(8,128)(2,1)} %bitcast.13, bf16[32,32,512]{2,1,0:T(8,128)(2,1)} %bitcast.9, bf16[32,32,512]{2,1,0:T(8,128)(2,1)} %copy-done.5), custom_call_target="tpu_custom_call" | custom-call | flops 4026531840 | bytes 2097152 | tf_op jit(solution)/shard_map/cost/pallas_call | solution.py:123
  56.0 0.8 fusion
  56.8 2.9 %collective-permute-start.2 = (bf16[3,1,8,8,128]{4,3,2,1,0:T(8,128)(2,1)S(1)}, bf16[3,1,8,8,128]{4,3,2,1,0:T(8,128)(2,1)S(1)}, u32[]{:S(2)}, u32[]{:S(2)}) collective-permute-start(bf16[3,1,8,8,128]{4,3,2,1,0:T(8,128)(2,1)S(1)} %get-tuple-element.5), channel_id=1, source_target_pairs={{1,0},{2,1},{3,2},{4,3},{5,4},{6,5},{7,6},{9,8},{10,9},{11,10},{12... | collective-permute-start | bytes 147464 | tf_op jit(solution)/shard_map/ppermute | solution.py:217
  59.7 2.7 %collective-permute-start.1 = (bf16[3,1,8,8,128]{4,3,2,1,0:T(8,128)(2,1)S(1)}, bf16[3,1,8,8,128]{4,3,2,1,0:T(8,128)(2,1)S(1)}, u32[]{:S(2)}, u32[]{:S(2)}) collective-permute-start(bf16[3,1,8,8,128]{4,3,2,1,0:T(8,128)(2,1)S(1)} %get-tuple-element.6), channel_id=1, source_target_pairs={{0,1},{1,2},{2,3},{3,4},{4,5},{5,6},{6,7},{8,9},{9,10},{10,11},{11... | collective-permute-start | bytes 147464 | tf_op jit(solution)/shard_map/ppermute | solution.py:216
  62.4 18.8 %cost.3.inner_ref = bf16[3,6,8,8,128]{4,3,2,1,0:T(8,128)(2,1)} custom-call(s32[3,10]{1,0:T(4,128)} %slot_ref.3, s16[8,3,10,8,128]{4,3,2,1,0:T(8,128)(2,1)} %copy-done.1, bf16[3,32,1024]{2,1,0:T(8,128)(2,1)} %bitcast.14, bf16[32,32,512]{2,1,0:T(8,128)(2,1)} %bitcast.10, bf16[32,32,512]{2,1,0:T(8,128)(2,1)} %copy-done.5), custom_call_target="tpu_custom_call" | custom-call | flops 12079595520 | bytes 2097152 | tf_op jit(solution)/shard_map/cost/pallas_call | solution.py:123
  81.2 0.0 collective-permute-done.2.after_ref
  81.2 0.0 copy-start.2
  81.2 0.0 collective-permute-done.1.before_ref
  81.2 0.6 copy-done.2
  81.8 0.0 copy-start.3
  81.8 0.6 copy-done.3
  82.4 3.5 %mix.1 = bf16[3,8,8,8,128]{4,3,2,1,0:T(8,128)(2,1)} custom-call(bf16[24,96]{1,0:T(8,128)(2,1)} %reshape.13.weight_ref, bf16[3,1,8,8,128]{4,3,2,1,0:T(8,128)(2,1)} %copy-done.3, bf16[3,2,8,8,128]{4,3,2,1,0:T(8,128)(2,1)} %cost.2.edge_ref, bf16[3,6,8,8,128]{4,3,2,1,0:T(8,128)(2,1)} %cost.3.inner_ref, bf16[3,1,8,8,128]{4,3,2,1,0:T(8,128)(2,1)} %copy-done.2), custom_call_target="tpu_custom_call" | custom-call | tf_op jit(solution)/shard_map/mix/pallas_call | solution.py:191
  (2 shorter events, 0.0 us)
Async XLA Ops:
  26.5 3.9 %copy-start = (bf16[16,2,32,512]{3,2,1,0:T(8,128)(2,1)}, bf16[16,2,32,512]{3,2,1,0:T(8,128)(2,1)S(1)}, u32[]{:S(2)}) copy-start(bf16[16,2,32,512]{3,2,1,0:T(8,128)(2,1)S(1)} %all_to_all.10) | copy-start | bytes 3145732
  26.5 17.7 %collective-permute-start = (bf16[32,32,512]{2,1,0:T(8,128)(2,1)S(1)}, bf16[32,32,512]{2,1,0:T(8,128)(2,1)S(1)}, u32[]{:S(2)}, u32[]{:S(2)}) collective-permute-start(bf16[32,32,512]{2,1,0:T(8,128)(2,1)S(1)} %bitcast.8), channel_id=1, source_target_pairs={{0,1},{1,0},{2,3},{3,2},{4,5},{5,4},{6,7},{7,6},{8,9},{9,8},{10,11... | collective-permute-start | bytes 3145736 | tf_op jit(solution)/shard_map/ppermute | solution.py:211
  30.4 4.8 %copy-start.4 = (bf16[27,8,8]{0,2,1:T(8,128)(2,1)S(1)}, bf16[27,8,8]{0,2,1:T(8,128)(2,1)}, u32[]{:S(2)}) copy-start(bf16[27,8,8]{0,2,1:T(8,128)(2,1)} %param.9) | copy-start | bytes 10372
  30.4 13.8 %all-to-all-start = ((s16[8,3,10,8,128]{4,3,2,1,0:T(8,128)(2,1)}), s16[8,3,10,8,128]{4,3,2,1,0:T(8,128)(2,1)S(1)}, u32[]{:S(2)}, u32[]{:S(2)}) async-start(s16[8,3,10,8,128]{4,3,2,1,0:T(8,128)(2,1)} %pack.1), calls=%async_computation | async-start | bytes 983040 | tf_op jit(solution)/shard_map/all_to_all | solution.py:213
  44.3 0.8 copy-start.1
  45.0 1.0 %copy-start.5 = (bf16[32,32,512]{2,1,0:T(8,128)(2,1)}, bf16[32,32,512]{2,1,0:T(8,128)(2,1)S(1)}, u32[]{:S(2)}) copy-start(bf16[32,32,512]{2,1,0:T(8,128)(2,1)S(1)} %collective-permute-done.far_ref) | copy-start | bytes 3145732
  56.8 24.3 %collective-permute-start.2 = (bf16[3,1,8,8,128]{4,3,2,1,0:T(8,128)(2,1)S(1)}, bf16[3,1,8,8,128]{4,3,2,1,0:T(8,128)(2,1)S(1)}, u32[]{:S(2)}, u32[]{:S(2)}) collective-permute-start(bf16[3,1,8,8,128]{4,3,2,1,0:T(8,128)(2,1)S(1)} %get-tuple-element.5), channel_id=1, source_target_pairs={{1,0},{2,1},{3,2},{4,3},{5,4},{6,5},{7,6},{9,8},{10,9},{11,10},{12... | collective-permute-start | bytes 147464 | tf_op jit(solution)/shard_map/ppermute | solution.py:217
  59.7 21.5 %collective-permute-start.1 = (bf16[3,1,8,8,128]{4,3,2,1,0:T(8,128)(2,1)S(1)}, bf16[3,1,8,8,128]{4,3,2,1,0:T(8,128)(2,1)S(1)}, u32[]{:S(2)}, u32[]{:S(2)}) collective-permute-start(bf16[3,1,8,8,128]{4,3,2,1,0:T(8,128)(2,1)S(1)} %get-tuple-element.6), channel_id=1, source_target_pairs={{0,1},{1,2},{2,3},{3,4},{4,5},{5,6},{6,7},{8,9},{9,10},{10,11},{11... | collective-permute-start | bytes 147464 | tf_op jit(solution)/shard_map/ppermute | solution.py:216
  81.2 0.6 copy-start.2
  81.8 0.6 copy-start.3
